TPU v7x, 32 devices: a whole 2x2x4 slice. The times are simulated.
32 devices in a mesh: row: 8 (over z, y), col: 4 (over x, core).
Axes of the slice: x: 2, y: 2, z: 4, core: 2. Of those that a mesh axis runs over, the one named last changes fastest.
Arguments:
- weights: bfloat16 [2, 8192, 8192], P(None, 'row', 'col'), may hold values from -0.0625 to 0.0625
- preact: float32 [2, 2, 8192], P(None, None, 'row'), may hold values from -2.5 to 2.5
- panel: bfloat16 [2, 64, 8192], P(None, None, 'col'), may hold values from -6 to 6
Outputs:
- basis_out: float32 [2, 64, 8192], P(None, None, 'col')
All inputs are finite; a program needn't handle non-finite values.
Results may differ from a plain program's by a relative error of at most 0.035.
Values may be sent and summed in bfloat16 or wider, within the bound.
A program may use at most 64 MiB of HBM per device.

v0:
```python
from functools import partial

import jax
import jax.numpy as jnp
from jax import lax
from jax.sharding import PartitionSpec as P

WIDTH = 8192
ITERS = 2


def on_device(weights, preact, panel):
    slopes = 1.0 - jnp.tanh(preact) ** 2
    layers = weights.shape[0]
    current = panel
    basis_out = panel.astype(jnp.float32)
    for iteration in range(ITERS):
        cotangent = None
        for layer_at in range(layers):
            partial_out = jnp.einsum(
                "bki,oi->bko", current, weights[layer_at], preferred_element_type=jnp.float32
            )
            summed = lax.psum_scatter(
                partial_out.astype(jnp.bfloat16), "col", scatter_dimension=1, tiled=True
            ).astype(jnp.float32)
            scaled = (slopes[:, layer_at, None, :] * summed).astype(jnp.bfloat16)
            if layer_at + 1 < layers:
                spread = lax.all_gather(scaled, "row", axis=2, tiled=True)
                current = lax.all_to_all(spread, "col", split_axis=2, concat_axis=1, tiled=True)
            else:
                cotangent = lax.all_gather(scaled, "col", axis=1, tiled=True)
        image_panel = None
        for layer_at in reversed(range(layers)):
            weighted = (slopes[:, layer_at, None, :] * cotangent).astype(jnp.bfloat16)
            partial_in = jnp.einsum(
                "bko,oi->bki", weighted, weights[layer_at], preferred_element_type=jnp.float32
            )
            if layer_at == 0:
                pieces = lax.psum_scatter(
                    partial_in.astype(jnp.bfloat16), "row", scatter_dimension=2, tiled=True
                )
                image_panel = lax.all_gather(pieces, "row", axis=2, tiled=True)
            else:
                pieces = lax.psum_scatter(
                    partial_in.astype(jnp.bfloat16), "row", scatter_dimension=1, tiled=True
                )
                spread = lax.all_gather(pieces, "col", axis=2, tiled=True)
                cotangent = lax.all_to_all(spread, "row", split_axis=2, concat_axis=1, tiled=True)
        local_gram = jnp.einsum(
            "bkw,bjw->bkj", image_panel, image_panel, preferred_element_type=jnp.float32
        )
        gram_sum = lax.psum(local_gram.astype(jnp.bfloat16), "col").astype(jnp.float32)
        factor = jnp.linalg.cholesky(gram_sum / WIDTH)
        basis_out = jax.vmap(partial(jax.scipy.linalg.solve_triangular, lower=True))(
            factor, image_panel.astype(jnp.float32)
        )
        current = basis_out.astype(jnp.bfloat16)
    return basis_out


def solution(mesh):
    return jax.shard_map(
        on_device,
        mesh=mesh,
        in_specs=(P(None, "row", "col"), P(None, None, "row"), P(None, None, "col")),
        out_specs=P(None, None, "col"),
        check_vma=False,
    )
```

profile of v0, /device:TPU:0, one launch (start us, length us, event | category | flops | bytes accessed | tf_op | source)
XLA Modules:
  0.0 776.8 jit_solution(17862595918340202358)
XLA Ops:
  12.1 22.8 %reduce-scatter.13.cloned.1.call-done = bf16[2,16,1024]{2,1,0:T(8,128)(2,1)} async-done(((bf16[2,64,1024]{2,1,0:T(8,128)(2,1)}), bf16[2,16,1024]{2,1,0:T(8,128)(2,1)}) %reduce-scatter.13.cloned.1.call-update) | async-done | bytes 65552 | tf_op jit(solution)/shard_map/reduce_scatter | solution.py:23
  35.8 31.6 %all_gather.24 = bf16[2,16,8192]{2,1,0:T(8,128)(2,1)S(1)} all-gather(bf16[2,16,1024]{2,1,0:T(8,128)(2,1)S(1)} %multiply_convert_fusion.7), channel_id=1, replica_groups=mesh['row'=8,'col'=4] {'row'}, dimensions={2}, use_global_device_ids=true | all-gather | bytes 589824 | tf_op jit(solution)/shard_map/all_gather | solution.py:28
  79.9 11.2 %all_to_all.54 = bf16[4,2,32768]{2,1,0:T(2,128)(2,1)S(1)} all-to-all(bf16[4,2,32768]{2,1,0:T(2,128)(2,1)S(1)} %reshape.23), channel_id=1, replica_groups=mesh['row'=8,'col'=4] {'col'}, dimensions={0} | all-to-all | bytes 1048576 | tf_op jit(solution)/shard_map/all_to_all | solution.py:29
  95.2 9.7 %copy.67 = bf16[2,16,4,2048]{3,2,1,0:T(4,128)(2,1)S(1)} copy(bf16[2,16,4,2048]{1,0,3,2:T(2,128)(2,1)} %bitcast.105) | data formatting | bytes 1048576 | tf_op jit(solution)/shard_map/all_to_all | solution.py:29
  109.7 20.0 %reduce-scatter.15.cloned.1.call-done = bf16[2,16,1024]{2,1,0:T(8,128)(2,1)} async-done(((bf16[2,64,1024]{2,1,0:T(8,128)(2,1)}), bf16[2,16,1024]{2,1,0:T(8,128)(2,1)}) %reduce-scatter.15.cloned.1.call-update) | async-done | bytes 65552 | tf_op jit(solution)/shard_map/reduce_scatter | solution.py:23
  140.9 63.2 %reduce-scatter.25.cloned.1.call-done = bf16[8,4096]{1,0:T(8,128)(2,1)} async-done(((bf16[64,4096]{1,0:T(8,128)(2,1)}), bf16[8,4096]{1,0:T(8,128)(2,1)}) %reduce-scatter.25.cloned.1.call-update) | async-done | bytes 65552
  227.8 9.0 %all-to-all-done.1 = bf16[8,2,8192]{2,1,0:T(2,128)(2,1)S(1)} async-done(((bf16[8,2,8192]{2,1,0:T(2,128)(2,1)}), bf16[8,2,8192]{2,1,0:T(2,128)(2,1)S(1)}, u32[]{:S(2)}, u32[]{:S(2)}) %all-to-all-start.1) | async-done | bytes 262176 | tf_op jit(solution)/shard_map/all_to_all | solution.py:48
  263.0 62.1 %reduce-scatter.17.cloned.1.call-done = bf16[2,64,256]{2,1,0:T(8,128)(2,1)} async-done(((bf16[2,64,2048]{2,1,0:T(8,128)(2,1)}), bf16[2,64,256]{2,1,0:T(8,128)(2,1)}) %reduce-scatter.17.cloned.1.call-update) | async-done | bytes 65552 | tf_op jit(solution)/shard_map/reduce_scatter | solution.py:39
  325.1 31.8 %all_gather.27 = bf16[2,64,2048]{2,1,0:T(8,128)(2,1)S(1)} all-gather(bf16[2,64,256]{2,1,0:T(8,128)(2,1)} %reduce-scatter.17.cloned.1.call-done), channel_id=1, replica_groups=mesh['row'=8,'col'=4] {'row'}, dimensions={2}, use_global_device_ids=true | all-gather | bytes 589824 | tf_op jit(solution)/shard_map/all_gather | solution.py:42
  357.2 10.3 %psum.14 = bf16[2,64,64]{1,2,0:T(8,128)(2,1)S(1)} all-reduce(bf16[2,64,64]{1,2,0:T(8,128)(2,1)S(1)} %convolution_convert_fusion.2), channel_id=1, replica_groups=mesh['row'=8,'col'=4] {'col'}, use_global_device_ids=true, to_apply=%region_4.0 | all-reduce | flops 8192 | bytes 32768 | tf_op jit(solution)/shard_map/psum | solution.py:52
  367.6 11.7 %custom-call.8 = f32[2,64,64]{2,1,0:T(8,128)S(1)} custom-call(f32[2,64,64]{2,1,0:T(8,128)S(1)} %fusion.62), custom_call_target="Cholesky" | custom-call | tf_op jit(solution)/shard_map/jit(cholesky)/cholesky | solution.py:53
  379.6 9.8 %custom-call.9 = f32[2,1,64,64]{2,3,1,0:T(8,128)S(1)} custom-call(f32[2,1,64,64]{3,2,1,0:T(8,128)S(1)} %select_bitcast_fusion.1), custom_call_target="InvertDiagBlocksLowerTriangular" | custom-call | tf_op jit(solution)/shard_map/vmap(jit(_solve_triangular))/triangular_solve | solution.py:54
  395.0 19.1 %reduce-scatter.19.cloned.1.call-done = bf16[2,16,1024]{2,1,0:T(8,128)(2,1)} async-done(((bf16[2,64,1024]{2,1,0:T(8,128)(2,1)}), bf16[2,16,1024]{2,1,0:T(8,128)(2,1)}) %reduce-scatter.19.cloned.1.call-update) | async-done | bytes 65552 | tf_op jit(solution)/shard_map/reduce_scatter | solution.py:23
  414.9 31.5 %all_gather.28 = bf16[2,16,8192]{2,1,0:T(8,128)(2,1)S(1)} all-gather(bf16[2,16,1024]{2,1,0:T(8,128)(2,1)S(1)} %multiply_convert_fusion.5), channel_id=1, replica_groups=mesh['row'=8,'col'=4] {'row'}, dimensions={2}, use_global_device_ids=true | all-gather | bytes 589824 | tf_op jit(solution)/shard_map/all_gather | solution.py:28
  458.8 11.2 %all_to_all.55 = bf16[4,2,32768]{2,1,0:T(2,128)(2,1)S(1)} all-to-all(bf16[4,2,32768]{2,1,0:T(2,128)(2,1)S(1)} %reshape.27), channel_id=1, replica_groups=mesh['row'=8,'col'=4] {'col'}, dimensions={0} | all-to-all | bytes 1048576 | tf_op jit(solution)/shard_map/all_to_all | solution.py:29
  474.2 9.7 %copy.68 = bf16[2,16,4,2048]{3,2,1,0:T(4,128)(2,1)S(1)} copy(bf16[2,16,4,2048]{1,0,3,2:T(2,128)(2,1)} %bitcast.107) | data formatting | bytes 1048576 | tf_op jit(solution)/shard_map/all_to_all | solution.py:29
  488.7 20.2 %reduce-scatter.21.cloned.1.call-done = bf16[2,16,1024]{2,1,0:T(8,128)(2,1)} async-done(((bf16[2,64,1024]{2,1,0:T(8,128)(2,1)}), bf16[2,16,1024]{2,1,0:T(8,128)(2,1)}) %reduce-scatter.21.cloned.1.call-update) | async-done | bytes 65552 | tf_op jit(solution)/shard_map/reduce_scatter | solution.py:23
  520.0 63.2 %reduce-scatter.27.cloned.1.call-done = bf16[8,4096]{1,0:T(8,128)(2,1)} async-done(((bf16[64,4096]{1,0:T(8,128)(2,1)}), bf16[8,4096]{1,0:T(8,128)(2,1)}) %reduce-scatter.27.cloned.1.call-update) | async-done | bytes 65552
  602.3 12.8 %all_to_all.56 = bf16[8,2,8192]{2,1,0:T(2,128)(2,1)S(1)} all-to-all(bf16[8,2,8192]{2,1,0:T(2,128)(2,1)S(1)} %reshape.29), channel_id=1, replica_groups=mesh['row'=8,'col'=4] {'row'}, dimensions={0} | all-to-all | bytes 524288 | tf_op jit(solution)/shard_map/all_to_all | solution.py:48
  641.3 62.3 %reduce-scatter.23.cloned.1.call-done = bf16[2,64,256]{2,1,0:T(8,128)(2,1)} async-done(((bf16[2,64,2048]{2,1,0:T(8,128)(2,1)}), bf16[2,64,256]{2,1,0:T(8,128)(2,1)}) %reduce-scatter.23.cloned.1.call-update) | async-done | bytes 65552 | tf_op jit(solution)/shard_map/reduce_scatter | solution.py:39
  703.6 31.6 %all_gather.31 = bf16[2,64,2048]{2,1,0:T(8,128)(2,1)S(1)} all-gather(bf16[2,64,256]{2,1,0:T(8,128)(2,1)} %reduce-scatter.23.cloned.1.call-done), channel_id=1, replica_groups=mesh['row'=8,'col'=4] {'row'}, dimensions={2}, use_global_device_ids=true | all-gather | bytes 589824 | tf_op jit(solution)/shard_map/all_gather | solution.py:42
  735.5 10.5 %psum.15 = bf16[2,64,64]{1,2,0:T(8,128)(2,1)S(1)} all-reduce(bf16[2,64,64]{1,2,0:T(8,128)(2,1)S(1)} %convolution_convert_fusion.1), channel_id=1, replica_groups=mesh['row'=8,'col'=4] {'col'}, use_global_device_ids=true, to_apply=%region_11.14 | all-reduce | flops 8192 | bytes 32768 | tf_op jit(solution)/shard_map/psum | solution.py:52
  746.2 11.7 %custom-call.10 = f32[2,64,64]{2,1,0:T(8,128)S(1)} custom-call(f32[2,64,64]{2,1,0:T(8,128)S(1)} %fusion.60), custom_call_target="Cholesky" | custom-call | tf_op jit(solution)/shard_map/jit(cholesky)/cholesky | solution.py:53
  758.1 9.8 %custom-call.11 = f32[2,1,64,64]{2,3,1,0:T(8,128)S(1)} custom-call(f32[2,1,64,64]{3,2,1,0:T(8,128)S(1)} %select_bitcast_fusion), custom_call_target="InvertDiagBlocksLowerTriangular" | custom-call | tf_op jit(solution)/shard_map/vmap(jit(_solve_triangular))/triangular_solve | solution.py:54
  (88 shorter events, 176.0 us)
Async XLA Ops:
  6.5 1.0 copy-start
  6.5 5.5 copy-start.2
  6.5 28.4 %reduce-scatter.13.cloned.1.call-start = ((), (), s32[]{:S(2)}) async-start(), calls=%async_computation.12 | async-start | bytes 327680 | tf_op jit(solution)/shard_map/reduce_scatter | solution.py:23
  12.0 117.8 %reduce-scatter.15.cloned.1.call-start = ((), (), s32[]{:S(2)}) async-start(), calls=%async_computation.13 | async-start | bytes 327680 | tf_op jit(solution)/shard_map/reduce_scatter | solution.py:23
  109.7 94.4 %reduce-scatter.25.cloned.1.call-start = ((), (), s32[]{:S(2)}) async-start(), calls=%async_computation.18 | async-start | bytes 589824
  223.8 13.1 %all-to-all-start.1 = ((bf16[8,2,8192]{2,1,0:T(2,128)(2,1)}), bf16[8,2,8192]{2,1,0:T(2,128)(2,1)S(1)}, u32[]{:S(2)}, u32[]{:S(2)}) async-start(bf16[8,2,8192]{2,1,0:T(2,128)(2,1)} %reshape.25), calls=%async_computation.3 | async-start | bytes 524288 | tf_op jit(solution)/shard_map/all_to_all | solution.py:48
  227.4 97.7 %reduce-scatter.17.cloned.1.call-start = ((), (), s32[]{:S(2)}) async-start(), calls=%async_computation.14 | async-start | bytes 589824 | tf_op jit(solution)/shard_map/reduce_scatter | solution.py:39
  262.9 151.1 %reduce-scatter.19.cloned.1.call-start = ((), (), s32[]{:S(2)}) async-start(), calls=%async_computation.15 | async-start | bytes 327680 | tf_op jit(solution)/shard_map/reduce_scatter | solution.py:23
  394.9 113.9 %reduce-scatter.21.cloned.1.call-start = ((), (), s32[]{:S(2)}) async-start(), calls=%async_computation.16 | async-start | bytes 327680 | tf_op jit(solution)/shard_map/reduce_scatter | solution.py:23
  488.6 94.6 %reduce-scatter.27.cloned.1.call-start = ((), (), s32[]{:S(2)}) async-start(), calls=%async_computation.19 | async-start | bytes 589824
  519.9 183.6 %reduce-scatter.23.cloned.1.call-start = ((), (), s32[]{:S(2)}) async-start(), calls=%async_computation.17 | async-start | bytes 589824 | tf_op jit(solution)/shard_map/reduce_scatter | solution.py:39
  637.5 132.5 %copy-start.1 = (bf16[2,64,2048]{2,1,0:T(8,128)(2,1)S(1)}, bf16[2,64,2048]{2,1,0:T(8,128)(2,1)}, u32[]{:S(2)}) copy-start(bf16[2,64,2048]{2,1,0:T(8,128)(2,1)} %param.8) | copy-start | bytes 1572868
Sparse Core Ops, SparseCore 0:
  12.1 22.7 reduce-scatter.12
  109.8 19.9 reduce-scatter.14
  141.0 63.0 reduce-scatter.24
  263.1 62.0 reduce-scatter.16
  395.0 18.9 reduce-scatter.18
  488.7 20.0 reduce-scatter.20
  520.1 63.1 reduce-scatter.26
  641.4 62.1 reduce-scatter.22
where the time goes:
time: 779 us; the launch traced here: 777 us
  waiting for transfers between devices  342 us (44%)
  blocking collectives  206 us (26%)
  local copies, waits for them, and re-layouts  114 us (15%)
  other arithmetic  62.1 us (8%)
  matrix products  34.7 us (4%)
  between operations  13.8 us (2%)
    unnamed x10, waiting for transfers between devices  127 us
    reduce_scatter x2, waiting for transfers between devices, on_device(): lax.psum_scatter(partial_in.astype(jnp.bfloat16), 'row', scatter_dimensio...  124 us
    reduce_scatter x4, waiting for transfers between devices, on_device(): lax.psum_scatter(partial_out.astype(jnp.bfloat16), 'col', scatter_dimensi...  82.1 us
    all_gather x2, blocking collectives, on_device(): image_panel = lax.all_gather(pieces, 'row', axis=2, tiled=True)  63.4 us
    all_gather x2, blocking collectives, on_device(): spread = lax.all_gather(scaled, 'row', axis=2, tiled=True)  63.1 us
    unnamed x24, local copies, waits for them, and re-layouts  49.6 us
    another operation x7, other arithmetic, on_device(): factor = jnp.linalg.cholesky(gram_sum / WIDTH)  23.8 us
    all_to_all x2, blocking collectives, on_device(): lax.all_to_all(spread, 'col', split_axis=2, concat_axis=1, tiled=True)  22.4 us
  transfers between devices with their start and end apart: 9, of which 9 were waited for; matrix products, arithmetic and copies ran while one was open for 0% of the time, Pallas kernels for 0%

commit v1 on v0

v1 whole, which is shorter than its diff:
```python
from functools import partial

import jax
import jax.numpy as jnp
from jax import lax
from jax.experimental import pallas as pl
from jax.experimental.pallas import tpu as pltpu
from jax.sharding import PartitionSpec as P

ITERS = 2
MESH = pl.DeviceIdType.MESH
F32, BF16 = jnp.float32, jnp.bfloat16


def plain_on_device(weights, preact, panel):
    width = panel.shape[2] * lax.axis_size("col")
    slopes = 1.0 - jnp.tanh(preact) ** 2
    layers = weights.shape[0]
    current = panel
    basis_out = panel.astype(F32)
    for iteration in range(ITERS):
        cotangent = None
        for layer_at in range(layers):
            partial_out = jnp.einsum("bki,oi->bko", current, weights[layer_at], preferred_element_type=F32)
            summed = lax.psum_scatter(
                partial_out.astype(BF16), "col", scatter_dimension=1, tiled=True
            ).astype(F32)
            scaled = (slopes[:, layer_at, None, :] * summed).astype(BF16)
            if layer_at + 1 < layers:
                spread = lax.all_gather(scaled, "row", axis=2, tiled=True)
                current = lax.all_to_all(spread, "col", split_axis=2, concat_axis=1, tiled=True)
            else:
                cotangent = lax.all_gather(scaled, "col", axis=1, tiled=True)
        image_panel = None
        for layer_at in reversed(range(layers)):
            weighted = (slopes[:, layer_at, None, :] * cotangent).astype(BF16)
            partial_in = jnp.einsum("bko,oi->bki", weighted, weights[layer_at], preferred_element_type=F32)
            if layer_at == 0:
                pieces = lax.psum_scatter(partial_in.astype(BF16), "row", scatter_dimension=2, tiled=True)
                image_panel = lax.all_gather(pieces, "row", axis=2, tiled=True)
            else:
                pieces = lax.psum_scatter(partial_in.astype(BF16), "row", scatter_dimension=1, tiled=True)
                spread = lax.all_gather(pieces, "col", axis=2, tiled=True)
                cotangent = lax.all_to_all(spread, "row", split_axis=2, concat_axis=1, tiled=True)
        local_gram = jnp.einsum("bkw,bjw->bkj", image_panel, image_panel, preferred_element_type=F32)
        gram_sum = lax.psum(local_gram.astype(BF16), "col").astype(F32)
        factor = jnp.linalg.cholesky(gram_sum / width)
        basis_out = jax.vmap(partial(jax.scipy.linalg.solve_triangular, lower=True))(
            factor, image_panel.astype(F32)
        )
        current = basis_out.astype(BF16)
    return basis_out


def inverse_factors(gram, inputs, rank, width):
    at_row = lax.broadcasted_iota(jnp.int32, (rank, 1), 0)
    row_at = lax.broadcasted_iota(jnp.int32, (rank, rank), 0)
    col_at = lax.broadcasted_iota(jnp.int32, (rank, rank), 1)
    eye = (row_at == col_at).astype(F32)
    joined = [
        jnp.concatenate([gram[:, b * rank:(b + 1) * rank], eye], axis=1) for b in range(inputs)
    ]
    for k in range(rank):
        for b in range(inputs):
            now = joined[b]
            pivot_row = now[k:k + 1, :]
            share = now[:, k:k + 1] / now[k:k + 1, k:k + 1]
            joined[b] = now - jnp.where(at_row > k, share, 0.0) * pivot_row
    inverses = []
    for b in range(inputs):
        diagonal = jnp.sum(joined[b][:, :rank] * eye, axis=1, keepdims=True)
        inverses.append(joined[b][:, rank:] * jnp.sqrt(width / diagonal))
    return inverses


def apply_inverse(inverse, panel):
    high = inverse.astype(BF16)
    low = (inverse - high.astype(F32)).astype(BF16)
    return jnp.dot(high, panel, preferred_element_type=F32) + jnp.dot(low, panel, preferred_element_type=F32)


def kernel(
    rows, cols, inputs, rank, out_block, in_block,
    w_hbm, preact_ref, panel_ref, out_ref,
    w, slopes, part_col, got_col, ring, spread, gathered_col, part_in, traded, sums,
    part_row, got_row, image, gram, w_sem, col_send, col_recv, row_send, row_recv,
    fwd_send, fwd_recv, sum_send, sum_recv,
):
    r, c = lax.axis_index("row"), lax.axis_index("col")
    n = inputs * rank
    layers = w.shape[0]
    per = rows // cols
    n_col, n_row = n // cols, n // rows
    width = cols * in_block
    per_input = cols // inputs
    my_input = c // per_input
    tile = 256

    loads = [pltpu.make_async_copy(w_hbm.at[l], w.at[l], w_sem.at[l]) for l in range(layers)]
    for load in loads:
        load.start()
    barrier = pltpu.get_barrier_semaphore()
    for d in range(1, rows):
        pl.semaphore_signal(barrier, inc=1, device_id={"row": lax.rem(r + d, rows)}, device_id_type=MESH)
    for d in range(1, cols):
        pl.semaphore_signal(barrier, inc=1, device_id={"col": lax.rem(c + d, cols)}, device_id_type=MESH)
    slopes[...] = 1.0 - jnp.tanh(preact_ref[...]) ** 2
    pl.semaphore_wait(barrier, rows + cols - 2)

    pending = []

    def trade(axis, source_of, into, send, recv):
        me, size = (r, rows) if axis == "row" else (c, cols)
        for d in range(1, size):
            peer = lax.rem(me + d, size)
            copy = pltpu.make_async_remote_copy(
                src_ref=source_of(peer), dst_ref=into.at[me], send_sem=send.at[d], recv_sem=recv.at[d],
                device_id={axis: peer}, device_id_type=MESH)
            copy.start()
            pending.append((None, copy))

        def arrive(d):
            origin = lax.rem(me + size - d, size)
            pltpu.make_async_remote_copy(
                src_ref=source_of(origin), dst_ref=into.at[origin], send_sem=send.at[d], recv_sem=recv.at[d],
                device_id={axis: origin}, device_id_type=MESH).wait_recv()
            return origin

        return arrive

    def forward(layer, pieces, into):
        def step(t, carry):
            at = pl.ds(pl.multiple_of(t * tile, tile), tile)
            total = None
            for lhs, low, high in pieces():
                term = lax.dot_general(
                    lhs, w[layer, at, low:high], (((1,), (1,)), ((), ())), preferred_element_type=F32)
                total = term if total is None else total + term
            into[:, :, at] = total.astype(BF16).reshape(cols, n_col, tile)
            return carry
        lax.fori_loop(0, out_block // tile, step, 0)

    def backward(layer, lhs_ref, store):
        def step(t, carry):
            at = pl.ds(pl.multiple_of(t * tile, tile), tile)
            store(t, jnp.dot(lhs_ref[...], w[layer, :, at], preferred_element_type=F32).astype(BF16))
            return carry
        lax.fori_loop(0, in_block // tile, step, 0)

    def weigh(layer, values_of, into):
        for b in range(inputs):
            into[b * rank:(b + 1) * rank, :] = (
                slopes[b * layers + layer:b * layers + layer + 1, :] * values_of(b)
            ).astype(BF16)

    def gathered_input(buf, b):
        return buf[b * per_input:(b + 1) * per_input].reshape(rank, out_block)

    def reduce_col(it, slot, part, got):
        arrive = trade("col", lambda peer: part.at[peer], got, col_send.at[it, slot], col_recv.at[it, slot])
        total = part[c].astype(F32)
        for d in range(1, cols):
            total = total + got[arrive(d)].astype(F32)
        return total

    def gather_col(it, slot, value, buf):
        buf[c] = value
        arrive = trade("col", lambda peer: buf.at[c], buf, col_send.at[it, slot], col_recv.at[it, slot])
        for d in range(1, cols):
            arrive(d)

    def factors(it):
        total = gram[it, 0]
        for at in range(1, cols):
            total = total + gram[it, at]
        return inverse_factors(total, inputs, rank, float(width))

    weighted = part_in.at[0]
    gram_arrive = None
    inverses = None
    for it in range(ITERS):
        first = panel_ref if it == 0 else None
        if it == 0:
            loads[0].wait()
        lhs = (lambda: [(panel_ref[...], 0, in_block)]) if it == 0 else (
            lambda: [(image[it - 1].reshape(n, in_block), 0, in_block)])
        for layer in range(layers):
            if it == 0 and layer > 0:
                loads[layer].wait()
            forward(layer, lhs, part_col.at[it, layer])
            summed = reduce_col(it, layer, part_col.at[it, layer], got_col.at[it, layer])
            my_slope = slopes[pl.ds(my_input * layers + layer, 1), :]
            if layer + 1 < layers:
                shards = ring.at[it, layer]
                shards[r] = (my_slope * summed).astype(BF16)
                arrive = trade("row", lambda peer: shards.at[r], shards,
                               row_send.at[it, layer], row_recv.at[it, layer])
                if it > 0 and layer == 0:
                    for d in range(1, cols):
                        gram_arrive(d)
                    inverses = factors(it - 1)
                blocks = spread.at[it, layer]
                for d in range(rows):
                    origin = arrive(d) if d else r
                    owner, at = origin // per, lax.rem(origin, per)
                    copy = pltpu.make_async_remote_copy(
                        src_ref=shards.at[origin], dst_ref=blocks.at[at, c],
                        send_sem=fwd_send.at[it, layer, d], recv_sem=fwd_recv.at[it, layer, at, c],
                        device_id={"col": owner}, device_id_type=MESH)

                    @pl.when(owner != c)
                    def _():
                        copy.start()

                    @pl.when(owner == c)
                    def _():
                        blocks[at, c] = shards[origin]
                    pending.append((owner != c, copy))
                for at in range(per):
                    for d in range(1, cols):
                        origin = lax.rem(c + d, cols)
                        pltpu.make_async_remote_copy(
                            src_ref=blocks.at[at, origin], dst_ref=blocks.at[at, origin],
                            send_sem=fwd_send.at[it, layer, 0], recv_sem=fwd_recv.at[it, layer, at, origin],
                            device_id={"col": origin}, device_id_type=MESH).wait_recv()
                lhs = lambda blocks=blocks: [
                    (blocks[at].reshape(n, out_block), at * out_block, (at + 1) * out_block) for at in range(per)]
            else:
                cot = gathered_col.at[it, layer]
                gather_col(it, layers, ((my_slope * summed) if it == 0 else summed).astype(BF16), cot)
        left = part_in.at[it]
        for layer in reversed(range(layers)):
            scaled = sums.at[it, layer]
            if layer == layers - 1 and it > 0:
                def values_of(b):
                    mixed = apply_inverse(inverses[b], gathered_input(cot, b))
                    slope = slopes[b * layers + layer:b * layers + layer + 1, :]
                    return (slope * mixed).astype(BF16).astype(F32)
            else:
                def values_of(b):
                    return gathered_input(cot, b).astype(F32)
            weigh(layer, values_of, scaled)
            if layer > 0:
                def store(t, value):
                    ratio = out_block // tile
                    at = pl.ds(pl.multiple_of(lax.rem(t, ratio) * tile, tile), tile)
                    left[layer, :, t // ratio, :, at] = value.reshape(cols, n_col, tile)
                backward(layer, scaled, store)
                whole = traded.at[it, layer, 0]
                got = traded.at[it, layer, 1]
                source = left.at[layer]
                arrive = trade("col", lambda peer: source.at[peer], whole,
                               col_send.at[it, layers + layer], col_recv.at[it, layers + layer])
                whole[c] = source[c]
                into = ring.at[it, layers - 1 + layer - 1] if False else got
                slots = into
                for d in range(cols):
                    owner = arrive(d) if d else c
                    for at in range(per):
                        target = owner * per + at
                        copy = pltpu.make_async_remote_copy(
                            src_ref=whole.at[owner, at],
                            dst_ref=slots.at[r // per, lax.rem(r, per)],
                            send_sem=sum_send.at[it, layer, d * per + at], recv_sem=sum_recv.at[it, layer, r],
                            device_id={"row": target}, device_id_type=MESH)

                        @pl.when(target != r)
                        def _():
                            copy.start()
                        pending.append((target != r, copy))
                total = whole[r // per, lax.rem(r, per)].astype(F32)
                for d in range(1, rows):
                    origin = lax.rem(r + d, rows)
                    place = slots.at[origin // per, lax.rem(origin, per)]
                    pltpu.make_async_remote_copy(
                        src_ref=place, dst_ref=place, send_sem=sum_send.at[it, layer, 0],
                        recv_sem=sum_recv.at[it, layer, origin],
                        device_id={"row": origin}, device_id_type=MESH).wait_recv()
                    total = total + place[...].astype(F32)
                cot = gathered_col.at[it, layer - 1]
                gather_col(it, 2 * layers + layer - 1, total.astype(BF16), cot)
            else:
                mine = part_row.at[it]

                def store(t, value):
                    mine[:, :, pl.ds(pl.multiple_of(t * tile, tile), tile)] = value.reshape(rows, n_row, tile)
                backward(layer, scaled, store)
                got = got_row.at[it]
                arrive = trade("row", lambda peer: mine.at[peer], got,
                               row_send.at[it, layers], row_recv.at[it, layers])
                total = mine[r].astype(F32)
                for d in range(1, rows):
                    total = total + got[arrive(d)].astype(F32)
                final = image.at[it]
                final[r] = total.astype(BF16)
                arrive = trade("row", lambda peer: final.at[r], final,
                               row_send.at[it, layers + 1], row_recv.at[it, layers + 1])
                for d in range(1, rows):
                    arrive(d)
        half = rows // inputs
        local = []
        for b in range(inputs):
            own = image[it, b * half:(b + 1) * half].reshape(rank, in_block)
            local.append(lax.dot_general(own, own, (((1,), (1,)), ((), ())), preferred_element_type=F32))
        gram[it, c] = jnp.concatenate(local, axis=1)
        here = gram.at[it]
        gram_arrive = trade("col", lambda peer, here=here: here.at[c], here,
                            col_send.at[it, 3 * layers], col_recv.at[it, 3 * layers])
    for d in range(1, cols):
        gram_arrive(d)
    inverses = factors(ITERS - 1)
    half = rows // inputs
    for b in range(inputs):
        own = image[ITERS - 1, b * half:(b + 1) * half].reshape(rank, in_block)
        out_ref[b * rank:(b + 1) * rank, :] = apply_inverse(inverses[b], own)
    for condition, copy in pending:
        if condition is None:
            copy.wait_send()
        else:
            @pl.when(condition)
            def _():
                copy.wait_send()


def on_device(rows, cols, weights, preact, panel):
    layers, out_block, in_block = weights.shape
    inputs, rank, _ = panel.shape
    n = inputs * rank
    per = rows // cols
    vm = pltpu.VMEM
    dma = pltpu.SemaphoreType.DMA
    scratch = [
        vm((layers, out_block, in_block), BF16),
        vm((inputs * layers, out_block), F32),
        vm((ITERS, layers, cols, n // cols, out_block), BF16),
        vm((ITERS, layers, cols, n // cols, out_block), BF16),
        vm((ITERS, layers - 1, rows, n // cols, out_block), BF16),
        vm((ITERS, layers - 1, per, cols, n // cols, out_block), BF16),
        vm((ITERS, layers, cols, n // cols, out_block), BF16),
        vm((ITERS, layers, cols, per, n // cols, out_block), BF16),
        vm((ITERS, layers, 2, cols, per, n // cols, out_block), BF16),
        vm((ITERS, layers, n, out_block), BF16),
        vm((ITERS, rows, n // rows, in_block), BF16),
        vm((ITERS, rows, n // rows, in_block), BF16),
        vm((ITERS, rows, n // rows, in_block), BF16),
        vm((ITERS, cols, rank, inputs * rank), F32),
        dma((layers,)),
        dma((ITERS, 3 * layers + 1, cols)), dma((ITERS, 3 * layers + 1, cols)),
        dma((ITERS, layers + 2, rows)), dma((ITERS, layers + 2, rows)),
        dma((ITERS, layers, rows)), dma((ITERS, layers, per, cols)),
        dma((ITERS, layers, rows)), dma((ITERS, layers, rows)),
    ]
    whole = pl.BlockSpec(memory_space=pltpu.VMEM)
    out = pl.pallas_call(
        partial(kernel, rows, cols, inputs, rank, out_block, in_block),
        out_shape=jax.ShapeDtypeStruct((n, in_block), F32),
        in_specs=[pl.BlockSpec(memory_space=pl.ANY), whole, whole],
        out_specs=whole,
        scratch_shapes=scratch,
        compiler_params=pltpu.CompilerParams(
            collective_id=0, has_side_effects=True, vmem_limit_bytes=56 * 1024 * 1024),
    )(weights, preact.reshape(inputs * layers, out_block), panel.reshape(n, in_block))
    return out.reshape(inputs, rank, in_block)


def solution(mesh):
    rows, cols = mesh.shape["row"], mesh.shape["col"]

    def body(weights, preact, panel):
        layers, out_block, in_block = weights.shape
        inputs, rank, _ = panel.shape
        n = inputs * rank
        fits = (
            rows % cols == 0 and cols % inputs == 0 and rows % inputs == 0
            and n % (16 * rows) == 0 and n % (16 * cols) == 0
            and out_block % 256 == 0 and rows * out_block == cols * in_block
        )
        if fits:
            return on_device(rows, cols, weights, preact, panel)
        return plain_on_device(weights, preact, panel)

    return jax.shard_map(
        body,
        mesh=mesh,
        in_specs=(P(None, "row", "col"), P(None, None, "row"), P(None, None, "col")),
        out_specs=P(None, None, "col"),
        check_vma=False,
    )
```

time: 779 us -> 190 us (0.24)
  waiting for transfers between devices: 342 us -> 0 us
  blocking collectives: 206 us -> 0 us
  Pallas kernels: 0 us -> 185 us
  local copies, waits for them, and re-layouts: 114 us -> 3.64 us
  other arithmetic: 62.1 us -> 0 us
  matrix products: 34.7 us -> 0 us
  between operations: 13.8 us -> 0.01 us
    reduce_scatter x6 -> x0, waiting for transfers between devices: 207 us -> none  [the longest x2 124 us: on_device(): lax.psum_scatter(partial_in.astype(jnp.bfloat16), 'row', scatter_dimensio...]
    pallas_call x0 -> x1, Pallas kernels: none -> 185 us  [on_device(): pl.pallas_call(partial(kernel, rows, cols, inputs, rank, out_block, in_bl...]
    all_gather x8 -> x0, blocking collectives: 150 us -> none  [the longest x2 63.4 us: on_device(): image_panel = lax.all_gather(pieces, 'row', axis=2, tiled=True)]
    unnamed x10 -> x0, waiting for transfers between devices: 127 us -> none
    unnamed x24 -> x1, local copies, waits for them, and re-layouts: 49.6 us -> 2.3 us
    another operation x12 -> x0, other arithmetic: 43.6 us -> none  [the longest x7 23.8 us: on_device(): factor = jnp.linalg.cholesky(gram_sum / WIDTH)]
    all_to_all x3 -> x0, blocking collectives: 35.2 us -> none  [the longest x2 22.4 us: on_device(): lax.all_to_all(spread, 'col', split_axis=2, concat_axis=1, tiled=True)]
    dot_general x10 -> x0, matrix products: 31.6 us -> none  [the longest x4 17.7 us: on_device(): jnp.einsum('bki,oi->bko', current, weights[layer_at], preferred_element_t...]
  transfers between devices with their start and end apart: 9 -> 0, of which waited for: 9 -> 0; matrix products, arithmetic and copies ran while one was open for 0% -> 0% of each run, Pallas kernels for 0% -> 0%
where the time goes in v1:
time: 190 us; the launch traced here: 189 us
  Pallas kernels  185 us (97%)
  local copies, waits for them, and re-layouts  3.64 us (2%)
    pallas_call x1, Pallas kernels, on_device(): pl.pallas_call(partial(kernel, rows, cols, inputs, rank, out_block, in_bl...  185 us

profile of v1, /device:TPU:0, one launch (start us, length us, event | category | flops | bytes accessed | tf_op | source)
XLA Modules:
  0.0 189.0 jit_solution(8385323481449725972)
XLA Ops:
  0.0 1.3 reshape.9.preact_ref
  1.3 185.4 %shard_map.37 = f32[128,2048]{1,0:T(8,128)} custom-call(bf16[2,1024,2048]{2,1,0:T(8,128)(2,1)} %w_hbm.1, f32[4,1024]{1,0:T(4,128)} %reshape.9.preact_ref, bf16[128,2048]{1,0:T(8,128)(2,1)} %bitcast.3), custom_call_target="tpu_custom_call" | custom-call | tf_op jit(solution)/shard_map/pallas_call | solution.py:354
  186.7 2.3 %copy.5 = f32[2,64,2048]{2,1,0:T(8,128)} copy(f32[2,64,2048]{2,1,0:T(8,128)} %bitcast.2) | data formatting | bytes 2097152

commit v2 on v0

v2 whole, which is shorter than its diff:
```python
from functools import partial

import jax
import jax.numpy as jnp
from jax import lax
from jax.experimental import pallas as pl
from jax.experimental.pallas import tpu as pltpu
from jax.sharding import PartitionSpec as P

ITERS = 2
MESH = pl.DeviceIdType.MESH
F32, BF16 = jnp.float32, jnp.bfloat16


def plain_on_device(weights, preact, panel):
    width = panel.shape[2] * lax.axis_size("col")
    slopes = 1.0 - jnp.tanh(preact) ** 2
    layers = weights.shape[0]
    current = panel
    basis_out = panel.astype(F32)
    for iteration in range(ITERS):
        cotangent = None
        for layer_at in range(layers):
            partial_out = jnp.einsum("bki,oi->bko", current, weights[layer_at], preferred_element_type=F32)
            summed = lax.psum_scatter(
                partial_out.astype(BF16), "col", scatter_dimension=1, tiled=True
            ).astype(F32)
            scaled = (slopes[:, layer_at, None, :] * summed).astype(BF16)
            if layer_at + 1 < layers:
                spread = lax.all_gather(scaled, "row", axis=2, tiled=True)
                current = lax.all_to_all(spread, "col", split_axis=2, concat_axis=1, tiled=True)
            else:
                cotangent = lax.all_gather(scaled, "col", axis=1, tiled=True)
        image_panel = None
        for layer_at in reversed(range(layers)):
            weighted = (slopes[:, layer_at, None, :] * cotangent).astype(BF16)
            partial_in = jnp.einsum("bko,oi->bki", weighted, weights[layer_at], preferred_element_type=F32)
            if layer_at == 0:
                pieces = lax.psum_scatter(partial_in.astype(BF16), "row", scatter_dimension=2, tiled=True)
                image_panel = lax.all_gather(pieces, "row", axis=2, tiled=True)
            else:
                pieces = lax.psum_scatter(partial_in.astype(BF16), "row", scatter_dimension=1, tiled=True)
                spread = lax.all_gather(pieces, "col", axis=2, tiled=True)
                cotangent = lax.all_to_all(spread, "row", split_axis=2, concat_axis=1, tiled=True)
        local_gram = jnp.einsum("bkw,bjw->bkj", image_panel, image_panel, preferred_element_type=F32)
        gram_sum = lax.psum(local_gram.astype(BF16), "col").astype(F32)
        factor = jnp.linalg.cholesky(gram_sum / width)
        basis_out = jax.vmap(partial(jax.scipy.linalg.solve_triangular, lower=True))(
            factor, image_panel.astype(F32)
        )
        current = basis_out.astype(BF16)
    return basis_out


def inverse_factors(gram, inputs, rank, width):
    at_row = lax.broadcasted_iota(jnp.int32, (rank, 1), 0)
    row_at = lax.broadcasted_iota(jnp.int32, (rank, rank), 0)
    col_at = lax.broadcasted_iota(jnp.int32, (rank, rank), 1)
    eye = (row_at == col_at).astype(F32)
    joined = [
        jnp.concatenate([gram[:, b * rank:(b + 1) * rank], eye], axis=1) for b in range(inputs)
    ]
    for k in range(rank):
        for b in range(inputs):
            now = joined[b]
            pivot_row = now[k:k + 1, :]
            share = now[:, k:k + 1] / now[k:k + 1, k:k + 1]
            joined[b] = now - jnp.where(at_row > k, share, 0.0) * pivot_row
    inverses = []
    for b in range(inputs):
        diagonal = jnp.sum(joined[b][:, :rank] * eye, axis=1, keepdims=True)
        inverses.append(joined[b][:, rank:] * jnp.sqrt(width / diagonal))
    return inverses


def apply_inverse(inverse, panel):
    high = inverse.astype(BF16)
    low = (inverse - high.astype(F32)).astype(BF16)
    return jnp.dot(high, panel, preferred_element_type=F32) + jnp.dot(low, panel, preferred_element_type=F32)


def kernel(
    rows, cols, inputs, rank, out_block, in_block, slices,
    w_hbm, preact_ref, panel_ref, out_ref,
    w, slopes, part_col, got_col, ring, spread, gathered_col, part_in, traded, summed_in, weighted,
    part_row, got_row, image, gram, w_sem, col_send, col_recv, row_send, row_recv,
    fwd_send, fwd_recv, sum_send, sum_recv,
):
    r, c = lax.axis_index("row"), lax.axis_index("col")
    layers = w.shape[0]
    per = rows // cols
    k_col, k_row = rank // cols, rank // slices
    pieces = rows // slices
    piece = in_block // pieces
    width = cols * in_block
    tile = 256

    loads = [pltpu.make_async_copy(w_hbm.at[l], w.at[l], w_sem.at[l]) for l in range(layers)]
    for load in loads:
        load.start()
    barrier = pltpu.get_barrier_semaphore()
    for d in range(1, rows):
        pl.semaphore_signal(barrier, inc=1, device_id={"row": lax.rem(r + d, rows)}, device_id_type=MESH)
    for d in range(1, cols):
        pl.semaphore_signal(barrier, inc=1, device_id={"col": lax.rem(c + d, cols)}, device_id_type=MESH)
    slopes[...] = 1.0 - jnp.tanh(preact_ref[...]) ** 2
    pl.semaphore_wait(barrier, rows + cols - 2)

    pending = []
    loaded = set()
    gram_arrivals = []
    inverses = {}

    def need(layer):
        if layer not in loaded:
            loaded.add(layer)
            loads[layer].wait()

    def trade(axis, source_of, place_of, send, recv):
        me, size = (r, rows) if axis == "row" else (c, cols)
        for d in range(1, size):
            peer = lax.rem(me + d, size)
            copy = pltpu.make_async_remote_copy(
                src_ref=source_of(peer), dst_ref=place_of(me), send_sem=send.at[d], recv_sem=recv.at[d],
                device_id={axis: peer}, device_id_type=MESH)
            copy.start()
            pending.append((None, copy))

        def arrive(d):
            origin = lax.rem(me + size - d, size)
            pltpu.make_async_remote_copy(
                src_ref=source_of(origin), dst_ref=place_of(origin), send_sem=send.at[d], recv_sem=recv.at[d],
                device_id={axis: origin}, device_id_type=MESH).wait_recv()
            return origin

        return arrive

    def forward(layer, lhs, into):
        need(layer)

        def step(t, carry):
            at = pl.ds(pl.multiple_of(t * tile, tile), tile)
            total = None
            for value, low, high in lhs():
                term = lax.dot_general(
                    value, w[layer, at, low:high], (((1,), (1,)), ((), ())), preferred_element_type=F32)
                total = term if total is None else total + term
            into[:, :, at] = total.astype(BF16).reshape(cols, k_col, tile)
            return carry
        lax.fori_loop(0, out_block // tile, step, 0)

    def backward(layer, lhs_ref, store):
        def step(t, carry):
            at = pl.ds(pl.multiple_of(t * tile, tile), tile)
            store(t, jnp.dot(lhs_ref[...], w[layer, :, at], preferred_element_type=F32).astype(BF16))
            return carry
        lax.fori_loop(0, in_block // tile, step, 0)

    def stream(b):
        for it in range(ITERS):
            if it == 0:
                lhs = lambda: [(panel_ref[b * rank:(b + 1) * rank, :], 0, in_block)]
            else:
                lhs = lambda: [
                    (image[b, it - 1, h].reshape(rank, piece), h * piece, (h + 1) * piece) for h in range(pieces)]
            for layer in range(layers):
                slope = slopes[b * layers + layer:b * layers + layer + 1, :]
                part, got = part_col.at[b, it, layer], got_col.at[b, it, layer]
                forward(layer, lhs, part)
                arrive = trade("col", lambda peer: part.at[peer], lambda me: got.at[me],
                               col_send.at[b, it, layer], col_recv.at[b, it, layer])
                yield
                total = part[c].astype(F32)
                for d in range(1, cols):
                    total = total + got[arrive(d)].astype(F32)
                if layer + 1 < layers:
                    shards, blocks = ring.at[b, it, layer], spread.at[b, it, layer]
                    shards[r] = (slope * total).astype(BF16)
                    arrive = trade("row", lambda peer: shards.at[r], lambda me: shards.at[me],
                                   row_send.at[b, it, layer], row_recv.at[b, it, layer])
                    if it > 0 and layer == 0 and b == inputs - 1:
                        finish_grams(it - 1)
                    yield
                    for d in range(rows):
                        origin = arrive(d) if d else r
                        owner, at = origin // per, lax.rem(origin, per)
                        copy = pltpu.make_async_remote_copy(
                            src_ref=shards.at[origin], dst_ref=blocks.at[at, c],
                            send_sem=fwd_send.at[b, it, layer, d], recv_sem=fwd_recv.at[b, it, layer, at, c],
                            device_id={"col": owner}, device_id_type=MESH)

                        @pl.when(owner != c)
                        def _():
                            copy.start()

                        @pl.when(owner == c)
                        def _():
                            blocks[at, c] = shards[origin]
                        pending.append((owner != c, copy))
                    yield
                    for at in range(per):
                        for d in range(1, cols):
                            origin = lax.rem(c + d, cols)
                            pltpu.make_async_remote_copy(
                                src_ref=blocks.at[at, origin], dst_ref=blocks.at[at, origin],
                                send_sem=fwd_send.at[b, it, layer, 0], recv_sem=fwd_recv.at[b, it, layer, at, origin],
                                device_id={"col": origin}, device_id_type=MESH).wait_recv()
                    lhs = lambda blocks=blocks: [
                        (blocks[at].reshape(rank, out_block), at * out_block, (at + 1) * out_block)
                        for at in range(per)]
                else:
                    cot = gathered_col.at[b, it, layer]
                    cot[c] = ((slope * total) if it == 0 else total).astype(BF16)
                    arrive = trade("col", lambda peer: cot.at[c], lambda me: cot.at[me],
                                   col_send.at[b, it, layers], col_recv.at[b, it, layers])
                    yield
                    for d in range(1, cols):
                        arrive(d)
            for layer in reversed(range(layers)):
                slope = slopes[b * layers + layer:b * layers + layer + 1, :]
                scaled = weighted.at[b, it, layer]
                value = cot[...].reshape(rank, out_block)
                if layer == layers - 1 and it > 0:
                    value = (slope * apply_inverse(inverses[it - 1][b], value)).astype(BF16)
                scaled[...] = (slope * value.astype(F32)).astype(BF16)
                if layer > 0:
                    whole, slots = traded.at[b, it, layer], summed_in.at[b, it, layer]
                    source = part_in.at[b, it, layer]

                    def store(t, value):
                        ratio = out_block // tile
                        at = pl.ds(pl.multiple_of(lax.rem(t, ratio) * tile, tile), tile)
                        source[:, t // ratio, :, at] = value.reshape(cols, k_col, tile)
                    backward(layer, scaled, store)
                    arrive = trade("col", lambda peer: source.at[peer], lambda me: whole.at[me],
                                   col_send.at[b, it, layers + layer], col_recv.at[b, it, layers + layer])
                    whole[c] = source[c]
                    yield
                    for d in range(cols):
                        owner = arrive(d) if d else c
                        for at in range(per):
                            target = owner * per + at
                            copy = pltpu.make_async_remote_copy(
                                src_ref=whole.at[owner, at], dst_ref=slots.at[r],
                                send_sem=sum_send.at[b, it, layer, d * per + at], recv_sem=sum_recv.at[b, it, layer, r],
                                device_id={"row": target}, device_id_type=MESH)

                            @pl.when(target != r)
                            def _():
                                copy.start()
                            pending.append((target != r, copy))
                    yield
                    total = whole[r // per, lax.rem(r, per)].astype(F32)
                    for d in range(1, rows):
                        origin = lax.rem(r + d, rows)
                        place = slots.at[origin]
                        pltpu.make_async_remote_copy(
                            src_ref=place, dst_ref=place, send_sem=sum_send.at[b, it, layer, 0],
                            recv_sem=sum_recv.at[b, it, layer, origin],
                            device_id={"row": origin}, device_id_type=MESH).wait_recv()
                        total = total + place[...].astype(F32)
                    cot = gathered_col.at[b, it, layer - 1]
                    cot[c] = total.astype(BF16)
                    arrive = trade("col", lambda peer: cot.at[c], lambda me: cot.at[me],
                                   col_send.at[b, it, 2 * layers + layer - 1],
                                   col_recv.at[b, it, 2 * layers + layer - 1])
                    yield
                    for d in range(1, cols):
                        arrive(d)
                else:
                    mine, got, final = part_row.at[b, it], got_row.at[b, it], image.at[b, it]

                    def store(t, value):
                        ratio = piece // tile
                        at = pl.ds(pl.multiple_of(lax.rem(t, ratio) * tile, tile), tile)
                        mine[t // ratio, :, :, at] = value.reshape(slices, k_row, tile)
                    backward(layer, scaled, store)

                    def shard(ref):
                        return lambda at: ref.at[at // slices, lax.rem(at, slices)]
                    arrive = trade("row", shard(mine), shard(got), row_send.at[b, it, layers], row_recv.at[b, it, layers])
                    yield
                    total = shard(mine)(r)[...].astype(F32)
                    for d in range(1, rows):
                        total = total + shard(got)(arrive(d))[...].astype(F32)
                    shard(final)(r)[...] = total.astype(BF16)
                    arrive = trade("row", lambda peer: shard(final)(r), shard(final),
                                   row_send.at[b, it, layers + 1], row_recv.at[b, it, layers + 1])
                    yield
                    for d in range(1, rows):
                        arrive(d)
            local = None
            for h in range(pieces):
                own = image[b, it, h].reshape(rank, piece)
                term = lax.dot_general(own, own, (((1,), (1,)), ((), ())), preferred_element_type=F32)
                local = term if local is None else local + term
            here = gram.at[b, it]
            here[c] = jnp.concatenate([local, local], axis=1)
            gram_arrivals.append((it, b, trade(
                "col", lambda peer, here=here: here.at[c], lambda me, here=here: here.at[me],
                col_send.at[b, it, 3 * layers], col_recv.at[b, it, 3 * layers])))

    def finish_grams(it):
        totals = {}
        for at, b, arrive in gram_arrivals:
            if at == it:
                for d in range(1, cols):
                    arrive(d)
                total = gram[b, it, 0]
                for d in range(1, cols):
                    total = total + gram[b, it, d]
                totals[b] = total[:, :rank]
        joint = jnp.concatenate([totals[b] for b in range(inputs)], axis=1)
        inverses[it] = inverse_factors(joint, inputs, rank, float(width))

    running = [stream(b) for b in range(inputs)]
    while running:
        for chain in list(running):
            try:
                next(chain)
            except StopIteration:
                running.remove(chain)
    finish_grams(ITERS - 1)
    for b in range(inputs):
        for h in range(pieces):
            own = image[b, ITERS - 1, h].reshape(rank, piece)
            out_ref[b * rank:(b + 1) * rank, h * piece:(h + 1) * piece] = apply_inverse(inverses[ITERS - 1][b], own)
    for condition, copy in pending:
        if condition is None:
            copy.wait_send()
        else:
            @pl.when(condition)
            def _():
                copy.wait_send()


def on_device(rows, cols, slices, weights, preact, panel):
    layers, out_block, in_block = weights.shape
    inputs, rank, _ = panel.shape
    per, pieces = rows // cols, rows // slices
    vm = pltpu.VMEM
    dma = pltpu.SemaphoreType.DMA
    many = (inputs, ITERS, layers)
    once = (inputs, ITERS)
    by_col = (cols, rank // cols, out_block)
    by_row = (pieces, slices, rank // slices, in_block // pieces)
    scratch = [
        vm((layers, out_block, in_block), BF16),
        vm((inputs * layers, out_block), F32),
        vm(many + by_col, BF16),
        vm(many + by_col, BF16),
        vm(many + (rows, rank // cols, out_block), BF16),
        vm(many + (per,) + by_col, BF16),
        vm(many + by_col, BF16),
        vm(many + (cols, per, rank // cols, out_block), BF16),
        vm(many + (cols, per, rank // cols, out_block), BF16),
        vm(many + (rows, rank // cols, out_block), BF16),
        vm(many + (rank, out_block), BF16),
        vm(once + by_row, BF16),
        vm(once + by_row, BF16),
        vm(once + by_row, BF16),
        vm(once + (cols, rank, 2 * rank), F32),
        dma((layers,)),
        dma(once + (3 * layers + 1, cols)), dma(once + (3 * layers + 1, cols)),
        dma(once + (layers + 2, rows)), dma(once + (layers + 2, rows)),
        dma(many + (rows,)), dma(many + (per, cols)),
        dma(many + (rows,)), dma(many + (rows,)),
    ]
    whole = pl.BlockSpec(memory_space=pltpu.VMEM)
    out = pl.pallas_call(
        partial(kernel, rows, cols, inputs, rank, out_block, in_block, slices),
        out_shape=jax.ShapeDtypeStruct((inputs * rank, in_block), F32),
        in_specs=[pl.BlockSpec(memory_space=pl.ANY), whole, whole],
        out_specs=whole,
        scratch_shapes=scratch,
        compiler_params=pltpu.CompilerParams(
            collective_id=0, has_side_effects=True, vmem_limit_bytes=56 * 1024 * 1024),
    )(weights, preact.reshape(inputs * layers, out_block), panel.reshape(inputs * rank, in_block))
    return out.reshape(inputs, rank, in_block)


def solution(mesh):
    rows, cols = mesh.shape["row"], mesh.shape["col"]

    def body(weights, preact, panel):
        layers, out_block, in_block = weights.shape
        inputs, rank, _ = panel.shape
        slices = max(rank // 16, 1)
        fits = (
            rows % cols == 0 and rows * out_block == cols * in_block and out_block % 256 == 0
            and rank % (16 * cols) == 0 and rows % slices == 0 and in_block % (256 * (rows // slices)) == 0
        )
        if fits:
            return on_device(rows, cols, slices, weights, preact, panel)
        return plain_on_device(weights, preact, panel)

    return jax.shard_map(
        body,
        mesh=mesh,
        in_specs=(P(None, "row", "col"), P(None, None, "row"), P(None, None, "col")),
        out_specs=P(None, None, "col"),
        check_vma=False,
    )
```

time: 779 us -> 166 us (0.21)
  waiting for transfers between devices: 342 us -> 0 us
  blocking collectives: 206 us -> 0 us
  Pallas kernels: 0 us -> 163 us
  local copies, waits for them, and re-layouts: 114 us -> 3.64 us
  other arithmetic: 62.1 us -> 0 us
  matrix products: 34.7 us -> 0 us
  between operations: 13.8 us -> 0.01 us
    reduce_scatter x6 -> x0, waiting for transfers between devices: 207 us -> none  [the longest x2 124 us: on_device(): lax.psum_scatter(partial_in.astype(jnp.bfloat16), 'row', scatter_dimensio...]
    pallas_call x0 -> x1, Pallas kernels: none -> 163 us  [on_device(): pl.pallas_call(partial(kernel, rows, cols, inputs, rank, out_block, in_bl...]
    all_gather x8 -> x0, blocking collectives: 150 us -> none  [the longest x2 63.4 us: on_device(): image_panel = lax.all_gather(pieces, 'row', axis=2, tiled=True)]
    unnamed x10 -> x0, waiting for transfers between devices: 127 us -> none
    unnamed x24 -> x1, local copies, waits for them, and re-layouts: 49.6 us -> 2.3 us
    another operation x12 -> x0, other arithmetic: 43.6 us -> none  [the longest x7 23.8 us: on_device(): factor = jnp.linalg.cholesky(gram_sum / WIDTH)]
    all_to_all x3 -> x0, blocking collectives: 35.2 us -> none  [the longest x2 22.4 us: on_device(): lax.all_to_all(spread, 'col', split_axis=2, concat_axis=1, tiled=True)]
    dot_general x10 -> x0, matrix products: 31.6 us -> none  [the longest x4 17.7 us: on_device(): jnp.einsum('bki,oi->bko', current, weights[layer_at], preferred_element_t...]
  transfers between devices with their start and end apart: 9 -> 0, of which waited for: 9 -> 0; matrix products, arithmetic and copies ran while one was open for 0% -> 0% of each run, Pallas kernels for 0% -> 0%
where the time goes in v2:
time: 166 us
  Pallas kernels  163 us (98%)
  local copies, waits for them, and re-layouts  3.64 us (2%)
    pallas_call x1, Pallas kernels, on_device(): pl.pallas_call(partial(kernel, rows, cols, inputs, rank, out_block, in_bl...  163 us

profile of v2, /device:TPU:0, one launch (start us, length us, event | category | flops | bytes accessed | tf_op | source)
XLA Modules:
  0.0 166.2 jit_solution(11330006315271467663)
XLA Ops:
  0.0 1.3 reshape.9.preact_ref
  1.3 162.5 %shard_map.37 = f32[128,2048]{1,0:T(8,128)} custom-call(bf16[2,1024,2048]{2,1,0:T(8,128)(2,1)} %w_hbm.1, f32[4,1024]{1,0:T(4,128)} %reshape.9.preact_ref, bf16[128,2048]{1,0:T(8,128)(2,1)} %bitcast.3), custom_call_target="tpu_custom_call" | custom-call | tf_op jit(solution)/shard_map/pallas_call | solution.py:370
  163.9 2.3 %copy.5 = f32[2,64,2048]{2,1,0:T(8,128)} copy(f32[2,64,2048]{2,1,0:T(8,128)} %bitcast.2) | data formatting | bytes 2097152

commit v3 on v2

--- a/solution.py
+++ b/solution.py
@@ -83,7 +83,7 @@
     rows, cols, inputs, rank, out_block, in_block, slices,
     w_hbm, preact_ref, panel_ref, out_ref,
     w, slopes, part_col, got_col, ring, spread, gathered_col, part_in, traded, summed_in, weighted,
-    part_row, got_row, image, gram, w_sem, col_send, col_recv, row_send, row_recv,
+    pair_in, send_in, part_row, pair_row, send_row, got_row, image, gram, w_sem, col_send, col_recv, row_send, row_recv,
     fwd_send, fwd_recv, sum_send, sum_recv,
 ):
     r, c = lax.axis_index("row"), lax.axis_index("col")
@@ -105,6 +105,48 @@
         pl.semaphore_signal(barrier, inc=1, device_id={"col": lax.rem(c + d, cols)}, device_id_type=MESH)
     slopes[...] = 1.0 - jnp.tanh(preact_ref[...]) ** 2
     pl.semaphore_wait(barrier, rows + cols - 2)
+
+    major, minor = r // per, lax.rem(r, per)
+
+    def push(source, place, send, recv, row, condition=None):
+        copy = pltpu.make_async_remote_copy(
+            src_ref=source, dst_ref=place, send_sem=send, recv_sem=recv,
+            device_id={"row": row}, device_id_type=MESH)
+        if condition is None:
+            copy.start()
+        else:
+            @pl.when(condition)
+            def _():
+                copy.start()
+        pending.append((condition, copy))
+
+    def landed(place, send, recv):
+        pltpu.make_async_remote_copy(
+            src_ref=place, dst_ref=place, send_sem=send, recv_sem=recv,
+            device_id={"row": r}, device_id_type=MESH).wait_recv()
+
+    def spread_rows(shard, send, recv, each=None):
+        for d in range(1, cols):
+            push(shard(r), shard(r), send.at[d], recv.at[d], lax.rem(major + d, cols) * per + minor)
+        for d in range(cols):
+            if d == 1:
+                yield
+            source = lax.rem(major + cols - d, cols) * per + minor
+            if d:
+                landed(shard(source), send.at[d], recv.at[d])
+            for e in range(1, per):
+                at = cols + d * per + e
+                push(shard(source), shard(source), send.at[at], recv.at[at], major * per + lax.rem(minor + e, per))
+            if each:
+                each(d * per, source)
+        yield
+        for d in range(cols):
+            for e in range(1, per):
+                at = cols + d * per + e
+                source = lax.rem(major + cols - d, cols) * per + lax.rem(minor + per - e, per)
+                landed(shard(source), send.at[at], recv.at[at])
+                if each:
+                    each(d * per + e, source)
 
     pending = []
     loaded = set()
@@ -176,13 +218,8 @@
                 if layer + 1 < layers:
                     shards, blocks = ring.at[b, it, layer], spread.at[b, it, layer]
                     shards[r] = (slope * total).astype(BF16)
-                    arrive = trade("row", lambda peer: shards.at[r], lambda me: shards.at[me],
-                                   row_send.at[b, it, layer], row_recv.at[b, it, layer])
-                    if it > 0 and layer == 0 and b == inputs - 1:
-                        finish_grams(it - 1)
-                    yield
-                    for d in range(rows):
-                        origin = arrive(d) if d else r
+
+                    def pass_on(d, origin):
                         owner, at = origin // per, lax.rem(origin, per)
                         copy = pltpu.make_async_remote_copy(
                             src_ref=shards.at[origin], dst_ref=blocks.at[at, c],
@@ -197,6 +234,14 @@
                         def _():
                             blocks[at, c] = shards[origin]
                         pending.append((owner != c, copy))
+
+                    steps = spread_rows(
+                        lambda at: shards.at[at], row_send.at[b, it, layer], row_recv.at[b, it, layer], pass_on)
+                    next(steps)
+                    if it > 0 and layer == 0 and b == inputs - 1:
+                        finish_grams(it - 1)
+                    yield
+                    yield from steps
                     yield
                     for at in range(per):
                         for d in range(1, cols):
@@ -236,29 +281,32 @@
                                    col_send.at[b, it, layers + layer], col_recv.at[b, it, layers + layer])
                     whole[c] = source[c]
                     yield
+                    pair, ready = pair_in.at[b, it, layer], send_in.at[b, it, layer]
+                    send, recv = sum_send.at[b, it, layer], sum_recv.at[b, it, layer]
                     for d in range(cols):
                         owner = arrive(d) if d else c
-                        for at in range(per):
-                            target = owner * per + at
-                            copy = pltpu.make_async_remote_copy(
-                                src_ref=whole.at[owner, at], dst_ref=slots.at[r],
-                                send_sem=sum_send.at[b, it, layer, d * per + at], recv_sem=sum_recv.at[b, it, layer, r],
-                                device_id={"row": target}, device_id_type=MESH)
-
-                            @pl.when(target != r)
-                            def _():
-                                copy.start()
-                            pending.append((target != r, copy))
-                    yield
-                    total = whole[r // per, lax.rem(r, per)].astype(F32)
-                    for d in range(1, rows):
-                        origin = lax.rem(r + d, rows)
-                        place = slots.at[origin]
-                        pltpu.make_async_remote_copy(
-                            src_ref=place, dst_ref=place, send_sem=sum_send.at[b, it, layer, 0],
-                            recv_sem=sum_recv.at[b, it, layer, origin],
-                            device_id={"row": origin}, device_id_type=MESH).wait_recv()
-                        total = total + place[...].astype(F32)
+                        for e in range(1, per):
+                            peer = lax.rem(minor + e, per)
+                            push(whole.at[owner, peer], pair.at[owner, e], send.at[d * per + e], recv.at[d * per + e],
+                                 major * per + peer)
+                    yield
+                    for d in range(cols):
+                        owner = lax.rem(c + cols - d, cols)
+                        total = whole[owner, minor].astype(F32)
+                        for e in range(1, per):
+                            landed(pair.at[owner, e], send.at[d * per + e], recv.at[d * per + e])
+                            total = total + pair[owner, e].astype(F32)
+                        ready[owner] = total.astype(BF16)
+                        push(ready.at[owner], slots.at[major], send.at[rows + d], recv.at[rows + major],
+                             owner * per + minor, owner != major)
+                    yield
+                    total = whole[major, minor].astype(F32)
+                    for e in range(1, per):
+                        total = total + pair[major, e].astype(F32)
+                    for d in range(1, cols):
+                        origin = lax.rem(major + d, cols)
+                        landed(slots.at[origin], send.at[rows], recv.at[rows + origin])
+                        total = total + slots[origin].astype(F32)
                     cot = gathered_col.at[b, it, layer - 1]
                     cot[c] = total.astype(BF16)
                     arrive = trade("col", lambda peer: cot.at[c], lambda me: cot.at[me],
@@ -278,17 +326,33 @@
 
                     def shard(ref):
                         return lambda at: ref.at[at // slices, lax.rem(at, slices)]
-                    arrive = trade("row", shard(mine), shard(got), row_send.at[b, it, layers], row_recv.at[b, it, layers])
-                    yield
-                    total = shard(mine)(r)[...].astype(F32)
-                    for d in range(1, rows):
-                        total = total + shard(got)(arrive(d))[...].astype(F32)
+                    pair, ready = pair_row.at[b, it], send_row.at[b, it]
+                    send, recv = row_send.at[b, it, layers], row_recv.at[b, it, layers]
+                    order = list(range(1, cols)) + [0]
+                    for d in order:
+                        to = lax.rem(major + d, cols)
+                        for e in range(1, per):
+                            peer = lax.rem(minor + e, per)
+                            push(shard(mine)(to * per + peer), pair.at[to, e], send.at[d * per + e],
+                                 recv.at[d * per + e], major * per + peer)
+                    yield
+                    for d in order:
+                        to = lax.rem(major + d, cols)
+                        total = shard(mine)(to * per + minor)[...].astype(F32)
+                        for e in range(1, per):
+                            landed(pair.at[to, e], send.at[d * per + e], recv.at[d * per + e])
+                            total = total + pair[to, e].astype(F32)
+                        if d:
+                            ready[to] = total.astype(BF16)
+                            push(ready.at[to], got.at[major], send.at[rows + d], recv.at[rows + d], to * per + minor)
+                    yield
+                    for d in range(1, cols):
+                        origin = lax.rem(major + cols - d, cols)
+                        landed(got.at[origin], send.at[rows + d], recv.at[rows + d])
+                        total = total + got[origin].astype(F32)
                     shard(final)(r)[...] = total.astype(BF16)
-                    arrive = trade("row", lambda peer: shard(final)(r), shard(final),
-                                   row_send.at[b, it, layers + 1], row_recv.at[b, it, layers + 1])
-                    yield
-                    for d in range(1, rows):
-                        arrive(d)
+                    yield from spread_rows(
+                        shard(final), row_send.at[b, it, layers + 1], row_recv.at[b, it, layers + 1])
             local = None
             for h in range(pieces):
                 own = image[b, it, h].reshape(rank, piece)
@@ -354,17 +418,21 @@
         vm(many + by_col, BF16),
         vm(many + (cols, per, rank // cols, out_block), BF16),
         vm(many + (cols, per, rank // cols, out_block), BF16),
-        vm(many + (rows, rank // cols, out_block), BF16),
+        vm(many + by_col, BF16),
         vm(many + (rank, out_block), BF16),
+        vm(many + (cols, per, rank // cols, out_block), BF16),
+        vm(many + by_col, BF16),
         vm(once + by_row, BF16),
-        vm(once + by_row, BF16),
+        vm(once + (cols, per) + by_row[2:], BF16),
+        vm(once + (cols,) + by_row[2:], BF16),
+        vm(once + (cols,) + by_row[2:], BF16),
         vm(once + by_row, BF16),
         vm(once + (cols, rank, 2 * rank), F32),
         dma((layers,)),
         dma(once + (3 * layers + 1, cols)), dma(once + (3 * layers + 1, cols)),
-        dma(once + (layers + 2, rows)), dma(once + (layers + 2, rows)),
+        dma(once + (layers + 2, rows + cols)), dma(once + (layers + 2, rows + cols)),
         dma(many + (rows,)), dma(many + (per, cols)),
-        dma(many + (rows,)), dma(many + (rows,)),
+        dma(many + (rows + cols,)), dma(many + (rows + cols,)),
     ]
     whole = pl.BlockSpec(memory_space=pltpu.VMEM)
     out = pl.pallas_call(

time: 166 us -> 160 us (0.964)
  Pallas kernels: 163 us -> 156 us
    pallas_call x1, Pallas kernels: 163 us -> 156 us  [on_device(): pl.pallas_call(partial(kernel, rows, cols, inputs, rank, out_block, in_bl...]
where the time goes in v3:
time: 160 us; the launch traced here: 159 us
  Pallas kernels  156 us (98%)
  local copies, waits for them, and re-layouts  3.64 us (2%)
    pallas_call x1, Pallas kernels, on_device(): pl.pallas_call(partial(kernel, rows, cols, inputs, rank, out_block, in_bl...  156 us

profile of v3, /device:TPU:0, one launch (start us, length us, event | category | flops | bytes accessed | tf_op | source)
XLA Modules:
  0.0 159.4 jit_solution(4301473628882514670)
XLA Ops:
  0.0 1.3 reshape.9.preact_ref
  1.3 155.7 %shard_map.37 = f32[128,2048]{1,0:T(8,128)} custom-call(bf16[2,1024,2048]{2,1,0:T(8,128)(2,1)} %w_hbm.1, f32[4,1024]{1,0:T(4,128)} %reshape.9.preact_ref, bf16[128,2048]{1,0:T(8,128)(2,1)} %bitcast.3), custom_call_target="tpu_custom_call" | custom-call | tf_op jit(solution)/shard_map/pallas_call | solution.py:438
  157.1 2.3 %copy.5 = f32[2,64,2048]{2,1,0:T(8,128)} copy(f32[2,64,2048]{2,1,0:T(8,128)} %bitcast.2) | data formatting | bytes 2097152
